TPU v7x, 256 devices: a whole 4x4x8 slice. The times are simulated.
256 devices in a mesh: seq: 64 (over x_hi, y, z), tp: 4 (over x_lo, core).
Axes of the slice: x: 4 (x_hi: 2, x_lo: 2; x = x_hi * 2 + x_lo), y: 4, z: 8, core: 2. Of those that a mesh axis runs over, the one named last changes fastest.
Arguments:
- features: bfloat16 [16384, 3, 4096], P('seq', None, 'tp'), may hold values from -6 to 6
- short_taps: float32 [3, 7, 4096], P(None, None, 'tp'), may hold values from -2 to 2
- residue: float32 [16, 4096], P(None, 'tp'), may hold values from -1.5 to 1.5
- decay_rate: float32 [16, 4096], P(None, 'tp'), may hold values from 6.1035157e-06 to 0.05
- w_out: bfloat16 [4096, 4096], P('tp', 'seq'), may hold values from -0.09375 to 0.09375
- cotangent: bfloat16 [16384, 4096], P('seq', 'tp'), may hold values from -16 to 16
Outputs:
- mixed: bfloat16 [16384, 4096], P('seq', 'tp')
- grad_features: bfloat16 [16384, 3, 4096], P('seq', None, 'tp')
- grad_weight: float32 [4096, 4096], P('tp', 'seq')
- grad_taps: float32 [3, 7, 4096], P(None, None, 'tp')
- grad_residue: float32 [16, 4096], P(None, 'tp')
- grad_log_rate: float32 [16, 4096], P(None, 'tp')
All inputs are finite; a program needn't handle non-finite values.
Results may differ from a plain program's by a relative error of at most 0.013.
Values may be sent and summed in bfloat16 or wider, within the bound.
No kernel may reach another device: no remote copies, remote signals or barrier semaphores. Data moves between devices by JAX's collectives and lax.ppermute only.
A program may use at most 128 MiB of HBM per device.

v0:
```python
import jax
import jax.numpy as jnp
from jax import lax
from jax.sharding import PartitionSpec as P


def shifted(array, axis, by):
    devices = lax.axis_size(axis)
    pairs = [(i, i + by) for i in range(devices) if 0 <= i + by < devices]
    return lax.ppermute(array, axis, pairs)


def pair_combine(earlier, later):
    return (earlier[0] * later[0], later[0] * earlier[1] + later[1])


def decay_prefix(values, rate_row):
    channels, length = values.shape
    block_len = min(128, length)
    block_count = length // block_len
    offsets = jnp.arange(block_len, dtype=jnp.float32)
    rising = jnp.exp(rate_row[:, None] * offsets[None, :])
    falling = jnp.exp(-rate_row[:, None] * offsets[None, :])
    shaped = values.reshape(channels, block_count, block_len) * rising[:, None, :]
    triangle = (offsets[:, None] <= offsets[None, :]).astype(jnp.float32)
    summed = jnp.einsum("cqs,st->cqt", shaped, triangle, precision=lax.Precision.HIGHEST)
    inside = summed * falling[:, None, :]
    factor = jnp.broadcast_to(jnp.exp(-rate_row * block_len)[:, None], (channels, block_count))
    _, running = lax.associative_scan(pair_combine, (factor, inside[:, :, -1]), axis=1)
    entering = jnp.concatenate([jnp.zeros((channels, 1), jnp.float32), running[:, :-1]], axis=1)
    carried = entering[:, :, None] * jnp.exp(
        -rate_row[:, None, None] * (offsets[None, None, :] + 1.0)
    )
    return (inside + carried).reshape(channels, length)


def modal_output(signal, rates, coeffs, starts):
    length = signal.shape[1]
    offsets = jnp.arange(length, dtype=jnp.float32)

    def one_mode(running_sum, params):
        rate_row, coeff_row, start_row = params
        states = decay_prefix(signal, rate_row) + start_row[:, None] * jnp.exp(
            -rate_row[:, None] * (offsets[None, :] + 1.0)
        )
        return (running_sum + coeff_row[:, None] * states, states)

    result, states_all = lax.scan(one_mode, jnp.zeros_like(signal), (rates, coeffs, starts))
    return (result, states_all)


def modal_grads(states_all, upstream, rates, coeffs, starts, finals):
    length = upstream.shape[1]
    offsets = jnp.arange(length, dtype=jnp.float32)

    def one_mode(running_sum, params):
        rate_row, coeff_row, start_row, final_row, states = params
        adjoint = jnp.flip(decay_prefix(jnp.flip(upstream, 1), rate_row), 1)
        adjoint = adjoint + final_row[:, None] * jnp.exp(
            -rate_row[:, None] * (length - offsets[None, :])
        )
        previous = jnp.concatenate([start_row[:, None], states[:, :-1]], axis=1)
        sums_pair = (jnp.sum(upstream * states, axis=1), jnp.sum(adjoint * previous, axis=1))
        return (running_sum + coeff_row[:, None] * adjoint, sums_pair)

    result, (alpha_rows, beta_rows) = lax.scan(
        one_mode, jnp.zeros_like(upstream), (rates, coeffs, starts, finals, states_all)
    )
    return (result, alpha_rows, beta_rows)


def coef_grads(alpha_rows, beta_rows, rates, residue):
    scales = jnp.sqrt(-jnp.expm1(-2.0 * rates))
    grad_res = scales * alpha_rows
    grad_log = rates * (
        alpha_rows * residue * jnp.exp(-2.0 * rates) / scales
        - jnp.exp(-rates) * residue * scales * beta_rows
    )
    return (grad_res, grad_log)


def local(features, short_taps, residue, decay_rate, w_out, cotangent):
    tok_count = features.shape[0]
    tap_reach = short_taps.shape[1] - 1
    earlier = shifted(features[tok_count - tap_reach :], "seq", 1)
    extended = jnp.concatenate([earlier, features], axis=0)
    mixed_in = short_taps[:, 0, :] * features
    for tap_index in range(1, tap_reach + 1):
        mixed_in = (
            mixed_in
            + short_taps[:, tap_index, :]
            * extended[tap_reach - tap_index : tap_reach - tap_index + tok_count]
        )
    query_part = mixed_in[:, 0, :]
    keyed = mixed_in[:, 1, :]
    valued = mixed_in[:, 2, :]
    product = (keyed * valued).astype(jnp.bfloat16)
    coeffs = residue * jnp.sqrt(-jnp.expm1(-2.0 * decay_rate))
    mode_count = residue.shape[0]
    chan_share = product.shape[1] // lax.axis_size("seq")
    first_channel = lax.axis_index("seq") * chan_share
    local_rates = lax.dynamic_slice_in_dim(decay_rate, first_channel, chan_share, 1)
    local_coeffs = lax.dynamic_slice_in_dim(coeffs, first_channel, chan_share, 1)
    local_residue = lax.dynamic_slice_in_dim(residue, first_channel, chan_share, 1)
    empty_state = jnp.zeros((mode_count, chan_share), jnp.float32)
    by_channel = lax.all_to_all(product.T, "seq", split_axis=0, concat_axis=1, tiled=True).astype(
        jnp.float32
    )
    conv_channels, mode_states = modal_output(by_channel, local_rates, local_coeffs, empty_state)
    convolved = lax.all_to_all(
        conv_channels.astype(jnp.bfloat16), "seq", split_axis=1, concat_axis=0, tiled=True
    ).T
    gated = (query_part * convolved).astype(jnp.bfloat16)
    full_weight = lax.all_gather(w_out, "seq", axis=1, tiled=True)
    partial_out = jnp.dot(gated, full_weight, preferred_element_type=jnp.float32)
    mixed = lax.psum_scatter(
        partial_out.astype(jnp.bfloat16), "tp", scatter_dimension=1, tiled=True
    )
    grad_rows = lax.all_gather(cotangent, "tp", axis=1, tiled=True)
    grad_gated = lax.dot_general(
        grad_rows, full_weight, (((1,), (1,)), ((), ())), preferred_element_type=jnp.float32
    ).astype(jnp.bfloat16)
    weight_term = lax.dot_general(
        gated, grad_rows, (((0,), (0,)), ((), ())), preferred_element_type=jnp.float32
    )
    grad_weight = lax.psum_scatter(weight_term, "seq", scatter_dimension=1, tiled=True)
    grad_conv = (grad_gated * query_part).astype(jnp.bfloat16)
    grad_channels = lax.all_to_all(
        grad_conv.T, "seq", split_axis=0, concat_axis=1, tiled=True
    ).astype(jnp.float32)
    back_channels, alpha_rows, beta_rows = modal_grads(
        mode_states, grad_channels, local_rates, local_coeffs, empty_state, empty_state
    )
    grad_product = lax.all_to_all(
        back_channels.astype(jnp.bfloat16), "seq", split_axis=1, concat_axis=0, tiled=True
    ).T
    local_res, local_log = coef_grads(alpha_rows, beta_rows, local_rates, local_residue)
    grad_residue, grad_log_rate = (
        lax.all_gather(local_res, "seq", axis=1, tiled=True),
        lax.all_gather(local_log, "seq", axis=1, tiled=True),
    )
    grad_query = grad_gated * convolved
    grad_key = (grad_product * valued).astype(jnp.bfloat16)
    grad_value = (grad_product * keyed).astype(jnp.bfloat16)
    grad_mixed_in = jnp.stack([grad_query, grad_key, grad_value], axis=1)
    later_rows = shifted(grad_mixed_in[:tap_reach], "seq", -1)
    grad_ext = jnp.concatenate([grad_mixed_in, later_rows], axis=0)
    grad_feat = short_taps[:, 0, :] * grad_mixed_in
    tap_terms = [
        jnp.einsum("tjc,tjc->jc", grad_mixed_in, features, preferred_element_type=jnp.float32)
    ]
    for tap_index in range(1, tap_reach + 1):
        grad_feat = (
            grad_feat + short_taps[:, tap_index, :] * grad_ext[tap_index : tap_index + tok_count]
        )
        tap_terms.append(
            jnp.einsum(
                "tjc,tjc->jc",
                grad_mixed_in,
                extended[tap_reach - tap_index : tap_reach - tap_index + tok_count],
                preferred_element_type=jnp.float32,
            )
        )
    tap_local = jnp.stack(tap_terms, axis=1)
    grad_taps = lax.psum(tap_local, "seq")
    return (
        mixed,
        grad_feat.astype(jnp.bfloat16),
        grad_weight,
        grad_taps,
        grad_residue,
        grad_log_rate,
    )


def solution(mesh):
    return jax.shard_map(
        local,
        mesh=mesh,
        in_specs=(
            P("seq", None, "tp"),
            P(None, None, "tp"),
            P(None, "tp"),
            P(None, "tp"),
            P("tp", "seq"),
            P("seq", "tp"),
        ),
        out_specs=(
            P("seq", "tp"),
            P("seq", None, "tp"),
            P("tp", "seq"),
            P(None, None, "tp"),
            P(None, "tp"),
            P(None, "tp"),
        ),
        check_vma=False,
    )
```

profile of v0, /device:TPU:6, one launch (start us, length us, event | category | flops | bytes accessed | tf_op | source)
XLA Modules:
  0.0 2036.1 jit_solution(4164407407298874918)
XLA Ops:
  30.4 13.2 all-gather.5.cloned.1.call-done
  43.6 154.6 %all-gather.3.cloned.1.call-done = bf16[1024,4096]{0,1:T(8,128)(2,1)} async-done(((bf16[1024,64]{0,1:T(8,128)(2,1)}), bf16[1024,4096]{0,1:T(8,128)(2,1)}) %all-gather.3.cloned.1.call-update) | async-done | bytes 8388624 | tf_op jit(solution)/shard_map/all_gather | solution.py:114
  208.0 10.5 all-to-all-start
  221.4 13.4 all-to-all-done
  241.9 183.7 %while.30 = (s32[]{:T(128)}, f32[16,16384]{1,0:T(8,128)}, f32[16,16,16384]{2,1,0:T(8,128)}, f32[16,16]{1,0:T(8,128)S(1)}, f32[16,16384]{1,0:T(8,128)S(1)}, /*ind...) while((s32[]{:T(128)}, f32[16,16384]{1,0:T(8,128)}, ...), condition=%wide.region_1.2_spmd.clone.clone, body=%wide.region_0.1_spmd.clone.clone.sunk | while | flops 406116288 | bytes 18331572 | solution.py:48
  427.7 13.2 all-to-all-start.1
  442.1 509.2 %while.29 = (s32[]{:T(128)}, f32[16,16384]{1,0:T(8,128)}, f32[16,16]{1,0:T(8,128)S(1)}, f32[16,16]{1,0:T(8,128)S(1)}, f32[16,16]{1,0:T(8,128)S(1)}, /*index=5*/f...) while((s32[]{:T(128)}, f32[16,16384]{1,0:T(8,128)}, ...), condition=%wide.region_6.7_spmd.clone, body=%wide.region_3.0_spmd.clone.sunk | while | flops 406378432 | bytes 24557768 | solution.py:66
  461.5 9.2 rev.12
  476.1 9.2 rev.11
  493.1 9.2 rev.12
  524.9 9.2 rev.12
  556.8 9.2 rev.12
  588.6 9.2 rev.12
  620.4 9.2 rev.12
  652.3 9.2 rev.12
  684.1 9.2 rev.12
  716.0 9.2 rev.12
  747.8 9.2 rev.12
  779.7 9.2 rev.12
  811.5 9.2 rev.12
  843.3 9.2 rev.12
  875.2 9.2 rev.12
  907.0 9.2 rev.12
  938.9 9.2 rev.12
  953.4 13.3 all-to-all-start.3
  968.8 12.4 all-to-all-done.3
  1000.5 9.9 fusion.47
  1017.0 177.2 %all_gather.14 = f32[16,1024]{0,1:T(8,128)S(1)} all-gather(f32[16,16]{0,1:T(8,128)S(1)} %get-tuple-element.307), channel_id=1, replica_groups=mesh['seq'=64,'tp'=4] {'seq'}, dimensions={1}, use_global_device_ids=true | all-gather | bytes 66560 | tf_op jit(solution)/shard_map/all_gather | solution.py:139
  1195.0 178.3 %all_gather.15 = f32[16,1024]{0,1:T(8,128)S(1)} all-gather(f32[16,16]{0,1:T(8,128)S(1)} %get-tuple-element.306), channel_id=1, replica_groups=mesh['seq'=64,'tp'=4] {'seq'}, dimensions={1}, use_global_device_ids=true | all-gather | bytes 66560 | tf_op jit(solution)/shard_map/all_gather | solution.py:140
  1378.0 219.9 %all-reduce.33.cloned.1.call-done = f32[3,7,1024]{2,0,1:T(4,128)} async-done(((f32[3,7,1024]{2,0,1:T(4,128)}), f32[3,7,1024]{2,0,1:T(4,128)}) %all-reduce.33.cloned.1.call-update) | async-done | bytes 86032 | tf_op jit(solution)/shard_map/psum | solution.py:165
  1599.5 26.1 %reduce-scatter.3.cloned.1.call-done = bf16[256,1024]{1,0:T(8,128)(2,1)} async-done(((bf16[256,4096]{1,0:T(8,128)(2,1)}), bf16[256,1024]{1,0:T(8,128)(2,1)}) %reduce-scatter.3.cloned.1.call-update) | async-done | bytes 524304 | tf_op jit(solution)/shard_map/reduce_scatter | solution.py:116
  1625.6 404.0 %reduce-scatter.5.cloned.1.call-done = f32[1024,64]{0,1:T(8,128)} async-done(((f32[1024,4096]{0,1:T(8,128)}), f32[1024,64]{0,1:T(8,128)}) %reduce-scatter.5.cloned.1.call-update) | async-done | bytes 262160 | tf_op jit(solution)/shard_map/reduce_scatter | solution.py:126
  (2541 shorter events, 612.5 us)
Async XLA Ops:
  7.2 36.4 %all-gather.5.cloned.1.call-start = ((), (), s32[]{:S(2)}) async-start(), calls=%async_computation.8 | async-start | bytes 2621440 | tf_op jit(solution)/shard_map/all_gather | solution.py:119
  7.9 190.3 %all-gather.3.cloned.1.call-start = ((), (), s32[]{:S(2)}) async-start(), calls=%async_computation.6 | async-start | bytes 8519680 | tf_op jit(solution)/shard_map/all_gather | solution.py:114
  9.5 13.1 collective-permute-start
  30.4 174.2 %copy-start = (f32[256,3,1024]{2,0,1:T(8,128)}, f32[256,3,1024]{2,0,1:T(8,128)S(1)}, u32[]{:S(2)}) copy-start(f32[256,3,1024]{2,0,1:T(8,128)S(1)} %multiply_add_fusion.15) | copy-start | bytes 9437188
  204.5 1.4 copy-start.10
  208.0 26.9 %all-to-all-start = ((bf16[64,16,256]{2,1,0:T(8,128)(2,1)}), bf16[64,16,256]{2,1,0:T(8,128)(2,1)S(1)}, u32[]{:S(2)}, u32[]{:S(2)}) async-start(bf16[64,16,256]{2,1,0:T(8,128)(2,1)} %bitcast.18), calls=%async_computation | async-start | bytes 1048576 | tf_op jit(solution)/shard_map/all_to_all | solution.py:106
  234.9 192.8 %all-to-all-start.2 = ((bf16[64,16,256]{2,1,0:T(8,128)(2,1)}), bf16[64,16,256]{2,1,0:T(8,128)(2,1)}, u32[]{:S(2)}, u32[]{:S(2)}) async-start(bf16[64,16,256]{2,1,0:T(8,128)(2,1)} %bitcast.25), calls=%async_computation.3 | async-start | bytes 1048576 | tf_op jit(solution)/shard_map/all_to_all | solution.py:128
  427.7 525.8 %all-to-all-start.1 = ((bf16[16,64,256]{2,0,1:T(8,128)(2,1)}), bf16[16,64,256]{2,0,1:T(8,128)(2,1)}, u32[]{:S(2)}, u32[]{:S(2)}) async-start(bf16[16,64,256]{2,0,1:T(8,128)(2,1)} %bitcast.189), calls=%async_computation.1 | async-start | bytes 1048576 | tf_op jit(solution)/shard_map/all_to_all | solution.py:110
  953.4 32.5 %copy-start.1 = (f32[256,3,1024]{2,0,1:T(8,128)S(1)}, f32[256,3,1024]{2,0,1:T(8,128)}, u32[]{:S(2)}) copy-start(f32[256,3,1024]{2,0,1:T(8,128)} %copy-done) | copy-start | bytes 9437188
  953.4 27.8 %all-to-all-start.3 = ((bf16[16,64,256]{2,0,1:T(8,128)(2,1)}), bf16[16,64,256]{2,0,1:T(8,128)(2,1)}, u32[]{:S(2)}, u32[]{:S(2)}) async-start(bf16[16,64,256]{2,0,1:T(8,128)(2,1)} %bitcast.291), calls=%async_computation.4 | async-start | bytes 1048576 | tf_op jit(solution)/shard_map/all_to_all | solution.py:134
  966.7 631.2 %all-reduce.33.cloned.1.call-start = ((), (), s32[]{:S(2)}) async-start(), calls=%async_computation.10 | async-start | bytes 229376 | tf_op jit(solution)/shard_map/psum | solution.py:165
  986.0 1.8 copy-start.9
  986.0 1.8 copy-start.11
  986.0 2.8 copy-start.8
  987.8 4.2 copy-start.4
  987.8 4.2 copy-start.6
  987.8 0.9 copy-start.2
  992.1 0.6 copy-start.12
  992.8 632.8 %reduce-scatter.3.cloned.1.call-start = ((), (), s32[]{:S(2)}) async-start(), calls=%async_computation.7 | async-start | bytes 2621440 | tf_op jit(solution)/shard_map/reduce_scatter | solution.py:116
  1000.2 1029.3 %reduce-scatter.5.cloned.1.call-start = ((), (), s32[]{:S(2)}) async-start(), calls=%async_computation.9 | async-start | bytes 17039360 | tf_op jit(solution)/shard_map/reduce_scatter | solution.py:126
  1010.4 1.0 copy-start.3
  1010.4 1.2 copy-start.5
  1010.4 1.4 copy-start.7
  1011.9 362.2 %collective-permute-start.1 = (bf16[6,3,1024]{2,0,1:T(8,128)(2,1)S(1)}, bf16[6,3,1024]{2,0,1:T(8,128)(2,1)S(1)}, u32[]{:S(2)}, u32[]{:S(2)}) collective-permute-start(bf16[6,3,1024]{2,0,1:T(8,128)(2,1)S(1)} %slice.600), channel_id=1, source_target_pairs={{4,0},{8,4},{12,8},{16,12},{20,16},{24,20},{28,24},{32,28},{36,32}... | collective-permute-start | bytes 110600 | tf_op jit(solution)/shard_map/ppermute | solution.py:10
Sparse Core Ops, SparseCore 0:
  9.8 33.7 all-gather.4
  47.3 150.7 all-gather.2
  992.9 604.9 all-reduce.32
  1601.0 24.4 reduce-scatter.2
  1628.5 400.9 reduce-scatter.4
where the time goes:
time: 2040 us
  waiting for transfers between devices  853 us (42%)
  local copies, waits for them, and re-layouts  456 us (22%)
  blocking collectives  355 us (17%)
  other arithmetic  252 us (12%)
  starting transfers between devices  53 us (3%)
  matrix products  45.4 us (2%)
    reduce_scatter x1, waiting for transfers between devices, local(): lax.psum_scatter(weight_term, 'seq', scatter_dimension=1, tiled=True)  404 us
    rev x32, local copies, waits for them, and re-layouts, one_mode(): adjoint = jnp.flip(decay_prefix(jnp.flip(upstream, 1), rate_row), 1)  294 us
    psum x1, waiting for transfers between devices, local(): grad_taps = lax.psum(tap_local, 'seq')  220 us
    all_gather x1, blocking collectives, local(): lax.all_gather(local_log, 'seq', axis=1, tiled=True)  178 us
    all_gather x1, blocking collectives, local(): lax.all_gather(local_res, 'seq', axis=1, tiled=True)  177 us
    all_gather x1, waiting for transfers between devices, local(): full_weight = lax.all_gather(w_out, 'seq', axis=1, tiled=True)  155 us
    slice x544, local copies, waits for them, and re-layouts, decay_prefix(): lax.associative_scan(pair_combine, (factor, inside[:, :, -1]), axis=1)  63.4 us
    reduce_sum x16, other arithmetic, one_mode(): jnp.sum(adjoint * previous, axis=1)  48.7 us
  transfers between devices with their start and end apart: 11, of which 8 were waited for; matrix products, arithmetic and copies ran while one was open for 36% of the time, Pallas kernels for 0%

commit v1 on v0

--- a/solution.py
+++ b/solution.py
@@ -162,7 +162,7 @@
             )
         )
     tap_local = jnp.stack(tap_terms, axis=1)
-    grad_taps = lax.psum(tap_local, "seq")
+    grad_taps = lax.all_gather(tap_local, "seq").sum(axis=0)
     return (
         mixed,
         grad_feat.astype(jnp.bfloat16),

time: 2040 us -> 1570 us (0.77)
  waiting for transfers between devices: 853 us -> 379 us
    reduce_scatter x1, waiting for transfers between devices: 404 us -> 175 us  [local(): lax.psum_scatter(weight_term, 'seq', scatter_dimension=1, tiled=True)]
    psum x1 -> x0, waiting for transfers between devices: 220 us -> none  [local(): grad_taps = lax.psum(tap_local, 'seq')]
    reduce_scatter x1, waiting for transfers between devices: 26.1 us -> 0.01 us  [local(): lax.psum_scatter(partial_out.astype(jnp.bfloat16), 'tp', scatter_dimensio...]
  transfers between devices with their start and end apart: 11 -> 11, of which waited for: 8 -> 6; matrix products, arithmetic and copies ran while one was open for 36% -> 47% of each run, Pallas kernels for 0% -> 0%
where the time goes in v1:
time: 1570 us
  local copies, waits for them, and re-layouts  454 us (29%)
  waiting for transfers between devices  379 us (24%)
  blocking collectives  357 us (23%)
  other arithmetic  256 us (16%)
  starting transfers between devices  52.9 us (3%)
  matrix products  45.3 us (3%)
    rev x32, local copies, waits for them, and re-layouts, one_mode(): adjoint = jnp.flip(decay_prefix(jnp.flip(upstream, 1), rate_row), 1)  294 us
    all_gather x1, blocking collectives, local(): lax.all_gather(local_log, 'seq', axis=1, tiled=True)  179 us
    all_gather x1, blocking collectives, local(): lax.all_gather(local_res, 'seq', axis=1, tiled=True)  178 us
    reduce_scatter x1, waiting for transfers between devices, local(): lax.psum_scatter(weight_term, 'seq', scatter_dimension=1, tiled=True)  175 us
    all_gather x1, waiting for transfers between devices, local(): full_weight = lax.all_gather(w_out, 'seq', axis=1, tiled=True)  155 us
    slice x544, local copies, waits for them, and re-layouts, decay_prefix(): lax.associative_scan(pair_combine, (factor, inside[:, :, -1]), axis=1)  63.4 us
    reduce_sum x16, other arithmetic, one_mode(): jnp.sum(adjoint * previous, axis=1)  49.2 us
    add x16, other arithmetic, one_mode(): return (running_sum + coeff_row[:, None] * states, states)  45.8 us
  transfers between devices with their start and end apart: 11, of which 6 were waited for; matrix products, arithmetic and copies ran while one was open for 47% of the time, Pallas kernels for 0%

profile of v1, /device:TPU:6, one launch (start us, length us, event | category | flops | bytes accessed | tf_op | source)
XLA Modules:
  0.0 1566.1 jit_solution(13879045894900150003)
XLA Ops:
  30.1 13.5 all-gather.7.cloned.1.call-done
  43.6 154.6 %all-gather.5.cloned.1.call-done = bf16[1024,4096]{0,1:T(8,128)(2,1)} async-done(((bf16[1024,64]{0,1:T(8,128)(2,1)}), bf16[1024,4096]{0,1:T(8,128)(2,1)}) %all-gather.5.cloned.1.call-update) | async-done | bytes 8388624 | tf_op jit(solution)/shard_map/all_gather | solution.py:114
  208.0 10.5 all-to-all-start
  221.4 13.5 all-to-all-done
  241.9 183.7 %while.30 = (s32[]{:T(128)}, f32[16,16384]{1,0:T(8,128)}, f32[16,16,16384]{2,1,0:T(8,128)}, f32[16,16]{1,0:T(8,128)S(1)}, f32[16,16384]{1,0:T(8,128)S(1)}, /*ind...) while((s32[]{:T(128)}, f32[16,16384]{1,0:T(8,128)}, ...), condition=%wide.region_1.2_spmd.clone.clone, body=%wide.region_0.1_spmd.clone.clone.sunk | while | flops 406116288 | bytes 18331572 | solution.py:48
  427.6 13.2 all-to-all-start.1
  442.1 509.6 %while.29 = (s32[]{:T(128)}, f32[16,16384]{1,0:T(8,128)}, f32[16,16]{1,0:T(8,128)S(1)}, f32[16,16]{1,0:T(8,128)S(1)}, f32[16,16]{1,0:T(8,128)S(1)}, /*index=5*/f...) while((s32[]{:T(128)}, f32[16,16384]{1,0:T(8,128)}, ...), condition=%wide.region_6.7_spmd.clone, body=%wide.region_3.0_spmd.clone.sunk | while | flops 406378432 | bytes 24557768 | solution.py:66
  444.5 9.2 rev.11
  461.5 9.2 rev.12
  493.1 9.2 rev.12
  507.9 9.2 rev.11
  524.9 9.2 rev.12
  539.8 9.2 rev.11
  556.8 9.2 rev.12
  588.7 9.2 rev.12
  620.5 9.2 rev.12
  652.4 9.2 rev.12
  684.3 9.2 rev.12
  716.2 9.2 rev.12
  748.0 9.2 rev.12
  779.9 9.2 rev.12
  811.8 9.2 rev.12
  843.6 9.2 rev.12
  875.5 9.2 rev.12
  907.4 9.2 rev.12
  939.3 9.2 rev.12
  953.9 13.3 all-to-all-start.3
  969.2 12.5 all-to-all-done.3
  1001.0 9.9 fusion.47
  1017.5 178.3 %all_gather.22 = f32[16,1024]{0,1:T(8,128)S(1)} all-gather(f32[16,16]{0,1:T(8,128)S(1)} %get-tuple-element.295), channel_id=1, replica_groups=mesh['seq'=64,'tp'=4] {'seq'}, dimensions={1}, use_global_device_ids=true | all-gather | bytes 66560 | tf_op jit(solution)/shard_map/all_gather | solution.py:139
  1196.6 178.7 %all_gather.23 = f32[16,1024]{0,1:T(8,128)S(1)} all-gather(f32[16,16]{0,1:T(8,128)S(1)} %get-tuple-element.294), channel_id=1, replica_groups=mesh['seq'=64,'tp'=4] {'seq'}, dimensions={1}, use_global_device_ids=true | all-gather | bytes 66560 | tf_op jit(solution)/shard_map/all_gather | solution.py:140
  1384.2 175.4 %reduce-scatter.5.cloned.1.call-done = f32[1024,64]{0,1:T(8,128)} async-done(((f32[1024,4096]{0,1:T(8,128)}), f32[1024,64]{0,1:T(8,128)}) %reduce-scatter.5.cloned.1.call-update) | async-done | bytes 262160 | tf_op jit(solution)/shard_map/reduce_scatter | solution.py:126
  (2540 shorter events, 596.9 us)
Async XLA Ops:
  7.2 36.4 %all-gather.7.cloned.1.call-start = ((), (), s32[]{:S(2)}) async-start(), calls=%async_computation.8 | async-start | bytes 2621440 | tf_op jit(solution)/shard_map/all_gather | solution.py:119
  7.9 190.3 %all-gather.5.cloned.1.call-start = ((), (), s32[]{:S(2)}) async-start(), calls=%async_computation.6 | async-start | bytes 8519680 | tf_op jit(solution)/shard_map/all_gather | solution.py:114
  9.5 13.1 collective-permute-start
  30.1 174.4 %copy-start = (f32[256,3,1024]{2,0,1:T(8,128)}, f32[256,3,1024]{2,0,1:T(8,128)S(1)}, u32[]{:S(2)}) copy-start(f32[256,3,1024]{2,0,1:T(8,128)S(1)} %multiply_add_fusion.15) | copy-start | bytes 9437188
  204.5 1.4 copy-start.10
  208.0 26.9 %all-to-all-start = ((bf16[64,16,256]{2,1,0:T(8,128)(2,1)}), bf16[64,16,256]{2,1,0:T(8,128)(2,1)S(1)}, u32[]{:S(2)}, u32[]{:S(2)}) async-start(bf16[64,16,256]{2,1,0:T(8,128)(2,1)} %bitcast.18), calls=%async_computation | async-start | bytes 1048576 | tf_op jit(solution)/shard_map/all_to_all | solution.py:106
  234.9 192.7 %all-to-all-start.2 = ((bf16[64,16,256]{2,1,0:T(8,128)(2,1)}), bf16[64,16,256]{2,1,0:T(8,128)(2,1)}, u32[]{:S(2)}, u32[]{:S(2)}) async-start(bf16[64,16,256]{2,1,0:T(8,128)(2,1)} %bitcast.25), calls=%async_computation.3 | async-start | bytes 1048576 | tf_op jit(solution)/shard_map/all_to_all | solution.py:128
  427.6 526.2 %all-to-all-start.1 = ((bf16[16,64,256]{2,0,1:T(8,128)(2,1)}), bf16[16,64,256]{2,0,1:T(8,128)(2,1)}, u32[]{:S(2)}, u32[]{:S(2)}) async-start(bf16[16,64,256]{2,0,1:T(8,128)(2,1)} %bitcast.176), calls=%async_computation.1 | async-start | bytes 1048576 | tf_op jit(solution)/shard_map/all_to_all | solution.py:110
  953.8 32.6 %copy-start.1 = (f32[256,3,1024]{2,0,1:T(8,128)S(1)}, f32[256,3,1024]{2,0,1:T(8,128)}, u32[]{:S(2)}) copy-start(f32[256,3,1024]{2,0,1:T(8,128)} %copy-done) | copy-start | bytes 9437188
  953.9 27.8 %all-to-all-start.3 = ((bf16[16,64,256]{2,0,1:T(8,128)(2,1)}), bf16[16,64,256]{2,0,1:T(8,128)(2,1)}, u32[]{:S(2)}, u32[]{:S(2)}) async-start(bf16[16,64,256]{2,0,1:T(8,128)(2,1)} %bitcast.279), calls=%async_computation.4 | async-start | bytes 1048576 | tf_op jit(solution)/shard_map/all_to_all | solution.py:134
  967.1 412.9 %all-gather.9.cloned.1.call-start = ((), (), s32[]{:S(2)}) async-start(), calls=%async_computation.10 | async-start | bytes 6389760 | tf_op jit(solution)/shard_map/all_gather | solution.py:165
  986.4 1.8 copy-start.9
  986.4 1.8 copy-start.11
  986.4 2.8 copy-start.8
  988.2 4.2 copy-start.4
  988.2 4.2 copy-start.6
  988.3 0.9 copy-start.2
  993.4 390.8 %reduce-scatter.3.cloned.1.call-start = ((), (), s32[]{:S(2)}) async-start(), calls=%async_computation.7 | async-start | bytes 2621440 | tf_op jit(solution)/shard_map/reduce_scatter | solution.py:116
  1000.7 558.9 %reduce-scatter.5.cloned.1.call-start = ((), (), s32[]{:S(2)}) async-start(), calls=%async_computation.9 | async-start | bytes 17039360 | tf_op jit(solution)/shard_map/reduce_scatter | solution.py:126
  1010.9 1.0 copy-start.3
  1010.9 1.2 copy-start.5
  1010.9 1.4 copy-start.7
  1012.4 363.7 %collective-permute-start.1 = (bf16[6,3,1024]{2,0,1:T(8,128)(2,1)S(1)}, bf16[6,3,1024]{2,0,1:T(8,128)(2,1)S(1)}, u32[]{:S(2)}, u32[]{:S(2)}) collective-permute-start(bf16[6,3,1024]{2,0,1:T(8,128)(2,1)S(1)} %slice.600), channel_id=1, source_target_pairs={{4,0},{8,4},{12,8},{16,12},{20,16},{24,20},{28,24},{32,28},{36,32}... | collective-permute-start | bytes 110600 | tf_op jit(solution)/shard_map/ppermute | solution.py:10
Sparse Core Ops, SparseCore 0:
  9.8 33.7 all-gather.6
  47.3 150.7 all-gather.4
  993.5 133.0 all-gather.8
  1129.5 27.1 reduce-scatter.2
  1159.9 399.6 reduce-scatter.4
